TPU v7x, 32 devices: a whole 2x2x4 slice. The times are simulated.
32 devices in a mesh: ctx: 16 (over z, x, core), tp: 2 (over y).
Axes of the slice: x: 2, y: 2, z: 4, core: 2. Of those that a mesh axis runs over, the one named last changes fastest.
Arguments:
- token_ids: int32 [8192], P('ctx'), may hold values from 0 to 511
- embed_table: bfloat16 [512, 8192], P(None, 'tp'), may hold values from -81 to 81
- projected_table: bfloat16 [512, 3, 8192], P(None, None, 'tp'), may hold values from -10.5 to 10.5
- feat_one: float32 [3, 3, 8192], P(None, None, 'tp'), may hold values from -3 to 3
- inner_taps: float32 [7, 8192], P(None, 'tp'), may hold values from -2 to 2
- feat_two: float32 [3, 3, 8192], P(None, None, 'tp'), may hold values from -3 to 3
- decay: float32 [8192, 16], P('tp'), may hold values from 3.540039e-05 to 0.03448276
- residue: float32 [8192, 16], P('tp'), may hold values from -0.26261287 to 0.26261287
Outputs:
- stream_out: bfloat16 [8192, 8192], P('ctx', 'tp')
All inputs are finite; a program needn't handle non-finite values.
Results may differ from a plain program's by a relative error of at most 0.0048.
Values may be sent and summed in bfloat16 or wider, within the bound.
A program may use at most 320 MiB of HBM per device.

v0:
```python
import math
import jax
import jax.numpy as jnp
from jax import lax
from jax.sharding import PartitionSpec as P

D = 8192
epsilon = 1e-06
PRECISE = lax.Precision.HIGHEST


def shifted(value, axis, steps):
    count = lax.axis_size(axis)
    first, last = (max(0, -steps), min(count, count - steps))
    return lax.ppermute(value, axis, [(source, source + steps) for source in range(first, last)])


def valid_taps(series, weights):
    tap_count = weights.shape[0]
    out_rows = series.shape[0] - tap_count + 1
    summed = weights[0] * series[tap_count - 1 : tap_count - 1 + out_rows]
    for offset in range(1, tap_count):
        summed = (
            summed
            + weights[offset] * series[tap_count - 1 - offset : tap_count - 1 - offset + out_rows]
        )
    return summed


def look_up(all_ids, embed_table, projected_table):
    vocab_size = embed_table.shape[0]
    one_hot = (all_ids[:, None] == jnp.arange(vocab_size, dtype=jnp.int32)[None, :]).astype(
        jnp.bfloat16
    )
    embedded = jnp.dot(one_hot, embed_table, preferred_element_type=jnp.float32)
    flattened = projected_table.reshape(vocab_size, -1)
    raw_rows = jnp.dot(one_hot, flattened, preferred_element_type=jnp.float32)
    return (embedded, raw_rows.reshape(all_ids.shape[0], 3, -1))


def block_one(raw_rows, embedded, feat_one, inner_taps):
    queries = valid_taps(raw_rows[:, 0], feat_one[:, 0])
    key_rows = valid_taps(raw_rows[:, 1], feat_one[:, 1])
    valued = valid_taps(raw_rows[:, 2], feat_one[:, 2])
    mixture = valid_taps(key_rows * valued, inner_taps)
    out_rows = mixture.shape[0]
    return (embedded + queries[queries.shape[0] - out_rows :] * mixture).astype(jnp.bfloat16)


def split_sizes(length):
    columns = 1
    for divisor in range(1, 129):
        if length % divisor == 0:
            columns = divisor
    return (2 * length // columns, columns)


def fourier_tables(outer_len, columns):
    total_len = outer_len * columns
    rows_k = jnp.arange(outer_len, dtype=jnp.int32)
    rows_q = jnp.arange(columns, dtype=jnp.int32)
    outer_angles = (rows_k[:, None] * rows_k[None, :] % outer_len).astype(jnp.float32) * (
        2.0 * math.pi / outer_len
    )
    col_angles = (rows_q[:, None] * rows_q[None, :] % columns).astype(jnp.float32) * (
        2.0 * math.pi / columns
    )
    tw_angles = (rows_k[:, None] * rows_q[None, :] % total_len).astype(jnp.float32) * (
        2.0 * math.pi / total_len
    )
    return (
        jnp.cos(outer_angles),
        -jnp.sin(outer_angles),
        jnp.cos(col_angles),
        -jnp.sin(col_angles),
        jnp.cos(tw_angles),
        -jnp.sin(tw_angles),
    )


def first_section(table, signal):
    if signal.dtype == jnp.bfloat16:
        upper = table.astype(jnp.bfloat16)
        lower = (table - upper.astype(jnp.float32)).astype(jnp.bfloat16)
        return jnp.einsum(
            "kp,bpq->bkq", upper, signal, preferred_element_type=jnp.float32
        ) + jnp.einsum("kp,bpq->bkq", lower, signal, preferred_element_type=jnp.float32)
    return jnp.einsum("kp,bpq->bkq", table, signal, precision=PRECISE)


def forward_transform(signal, tables):
    outer_re, outer_im, col_re, col_im, tw_re, tw_im = tables
    half_rows = signal.shape[1]
    first_re = first_section(outer_re[:, :half_rows], signal)
    first_im = first_section(outer_im[:, :half_rows], signal)
    turned_re = first_re * tw_re - first_im * tw_im
    turned_im = first_re * tw_im + first_im * tw_re
    out_re = jnp.einsum("bkq,ql->bkl", turned_re, col_re, precision=PRECISE) - jnp.einsum(
        "bkq,ql->bkl", turned_im, col_im, precision=PRECISE
    )
    out_im = jnp.einsum("bkq,ql->bkl", turned_re, col_im, precision=PRECISE) + jnp.einsum(
        "bkq,ql->bkl", turned_im, col_re, precision=PRECISE
    )
    return (out_re, out_im)


def inverse_transform(spec_re, spec_im, tables):
    outer_re, outer_im, col_re, col_im, tw_re, tw_im = tables
    outer_len = outer_re.shape[0]
    total_len = outer_len * col_re.shape[0]
    half_rows = outer_len // 2
    back_re = jnp.einsum("bkl,lq->bkq", spec_re, col_re, precision=PRECISE) + jnp.einsum(
        "bkl,lq->bkq", spec_im, col_im, precision=PRECISE
    )
    back_im = jnp.einsum("bkl,lq->bkq", spec_im, col_re, precision=PRECISE) - jnp.einsum(
        "bkl,lq->bkq", spec_re, col_im, precision=PRECISE
    )
    turn_re = back_re * tw_re + back_im * tw_im
    turn_im = back_im * tw_re - back_re * tw_im
    result = jnp.einsum(
        "pk,bkq->bpq", outer_re[:half_rows], turn_re, precision=PRECISE
    ) + jnp.einsum("pk,bkq->bpq", outer_im[:half_rows], turn_im, precision=PRECISE)
    return result / total_len


def causal_convolve(series, response):
    channels, length = series.shape
    outer_len, columns = split_sizes(length)
    tables = fourier_tables(outer_len, columns)
    half_rows = outer_len // 2
    sig_re, sig_im = forward_transform(series.reshape(channels, half_rows, columns), tables)
    fil_re, fil_im = forward_transform(response.reshape(channels, half_rows, columns), tables)
    prod_re = sig_re * fil_re - sig_im * fil_im
    prod_im = sig_re * fil_im + sig_im * fil_re
    return inverse_transform(prod_re, prod_im, tables).reshape(channels, length)


def mode_response(decay, residue, length, offset):
    positions = jnp.arange(length, dtype=jnp.int32).astype(jnp.float32) + offset

    def add_mode(mode_number, summed):
        decay_col = lax.dynamic_slice_in_dim(decay, mode_number, 1, 1)
        weight_col = lax.dynamic_slice_in_dim(residue, mode_number, 1, 1)
        return summed + weight_col * jnp.exp(-decay_col * positions[None, :])

    return lax.fori_loop(
        0, decay.shape[1], add_mode, jnp.zeros((decay.shape[0], length), jnp.float32)
    )


def on_device(
    token_ids, embed_table, projected_table, feat_one, inner_taps, feat_two, decay, residue
):
    tok_rows = token_ids.shape[0]
    channels = embed_table.shape[1]
    lead_one = feat_one.shape[0] - 1 + inner_taps.shape[0] - 1
    lead_two = feat_two.shape[0] - 1
    embedded, raw_rows = look_up(token_ids, embed_table, projected_table)
    raw_sent = raw_rows[tok_rows - lead_one :].astype(jnp.bfloat16)
    earlier = shifted(raw_sent, "ctx", 1)
    raw_ext = jnp.concatenate([earlier.astype(jnp.float32), raw_rows], axis=0)
    stream = block_one(raw_ext, embedded, feat_one, inner_taps)
    before = shifted(stream[tok_rows - lead_two :], "ctx", 1)
    stream_ext = jnp.concatenate([before, stream], axis=0)
    widened = stream_ext.astype(jnp.float32)
    squares = lax.psum(jnp.sum(widened * widened, axis=1), "tp")
    normed = widened * lax.rsqrt(squares / D + epsilon)[:, None]
    queries = valid_taps(normed, feat_two[:, 0])
    key_rows = valid_taps(normed, feat_two[:, 1])
    valued = valid_taps(normed, feat_two[:, 2])
    product = jnp.transpose(key_rows * valued).astype(jnp.bfloat16)
    per_device = channels // lax.axis_size("ctx")
    gathered = lax.all_to_all(product, "ctx", split_axis=0, concat_axis=1, tiled=True)
    first_lane = lax.axis_index("ctx") * per_device
    my_decay = lax.dynamic_slice_in_dim(decay, first_lane, per_device, 0)
    my_residue = lax.dynamic_slice_in_dim(residue, first_lane, per_device, 0)
    response = mode_response(my_decay, my_residue, gathered.shape[1], 0.0)
    convolved = causal_convolve(gathered, response)
    carried = lax.all_to_all(convolved, "ctx", split_axis=1, concat_axis=0, tiled=True)
    mixed_out = queries * jnp.transpose(carried)
    return (widened[lead_two:] + mixed_out).astype(jnp.bfloat16)


def solution(mesh):
    placed = (
        P("ctx"),
        P(None, "tp"),
        P(None, None, "tp"),
        P(None, None, "tp"),
        P(None, "tp"),
        P(None, None, "tp"),
        P("tp", None),
        P("tp", None),
    )
    return jax.shard_map(
        on_device, mesh=mesh, in_specs=placed, out_specs=P("ctx", "tp"), check_vma=False
    )
```

profile of v0, /device:TPU:15, one launch (start us, length us, event | category | flops | bytes accessed | tf_op | source)
XLA Modules:
  0.0 1082.3 jit_solution(17847357074202862382)
XLA Ops:
  16.7 20.7 %fusion.72 = f32[512,12288]{1,0:T(8,128)} fusion(bf16[512,12288]{0,1:T(8,128)(2,1)} %bitcast.240, s32[512]{0:T(512)S(1)} %copy-done.9), kind=kOutput, calls=%fused_computation.119 | convolution fusion | flops 6442713088 | bytes 37750784 | tf_op jit(solution)/shard_map/dot_general | solution.py:37
  44.1 100.5 %while.14 = (s32[]{:T(128)}, f32[256,8192]{1,0:T(8,128)}, f32[256,16]{0,1:T(8,128)S(1)}, f32[256,16]{0,1:T(8,128)S(1)}, s32[]{:T(128)}, /*index=5*/s32[]{:T(128)}) while((s32[]{:T(128)}, f32[256,8192]{1,0:T(8,128)}, f32[256,16]{0,1:T(8,128)S(1)}, f32[256,16]{0,1:T(8,128)S(1)}, s32[]{:T(128)}, /*index=5*/s32[]{:T(128)}) %tuple.64), condition=%wide.region_3.0_spmd.clone, body=%wide.region_2.0_spmd.clone.sunk | while | flops 8397059 | bytes 16848984 | solution.py:146
  152.9 29.2 %fusion.100 = f32[256,128,128]{2,1,0:T(8,128)} fusion(f32[256,64,128]{2,1,0:T(8,128)S(1)} %bitcast.238, f32[128,128]{0,1:T(8,128)S(1)} %sine_negate_fusion.1), kind=kOutput, calls=%fused_computation.158 | convolution fusion | flops 3221225472 | bytes 25198592 | tf_op jit(solution)/shard_map/kp,bpq->bkq/dot_general | solution.py:88
  182.1 24.7 %copy.73 = f32[512,12288]{0,1:T(8,128)} copy(f32[512,12288]{1,0:T(8,128)} %fusion.72) | data formatting | bytes 50331648 | tf_op jit(solution)/shard_map/dot_general | solution.py:37
  206.8 25.0 %copy.74 = f32[512,3,4096]{2,0,1:T(8,128)} copy(f32[512,3,4096]{0,2,1:T(8,128)} %bitcast.241) | data formatting | bytes 50331648 | tf_op jit(solution)/shard_map/reshape | solution.py:38
  250.2 21.3 %fusion.19 = f32[518,4096]{1,0:T(8,128)} fusion(f32[512,3,4096]{2,0,1:T(8,128)} %copy.74, f32[8,3,4096]{2,0,1:T(8,128)S(1)} %convert_element_type.123, f32[4096]{0:T(1024)S(1)} %bitcast.253, f32[4096]{0:T(1024)S(1)} %bitcast.254, f32[4096]{0:T(1024)S(1)} %bitcast.249, f32[4096]{0:T(1024)S(1)} %bitcast.250, f32[4096]{0:T(1024)S(1)} %bitcast.251, ...), kind=kLoop, calls=%fused_computation.56 | loop fusion | flops 36069376 | bytes 34144256 | tf_op jit(solution)/shard_map/mul | solution.py:45
  271.5 36.9 %fusion.46 = bf16[512,4096]{1,0:T(8,128)(2,1)} fusion(f32[518,4096]{1,0:T(8,128)} %fusion.19, f32[518,4096]{1,0:T(8,128)} %get-tuple-element.130, f32[518,4096]{1,0:T(8,128)} %get-tuple-element.131, f32[518,4096]{1,0:T(8,128)} %get-tuple-element.129, bf16[512,4096]{1,0:T(8,128)(2,1)} %param.11, f32[4096]{0:T(1024)S(1)} %bitcast.272, ...), kind=kOutput, calls=%fused_computation.87 | convolution fusion | flops 2191785984 | bytes 92440576 | tf_op jit(solution)/shard_map/dot_general | solution.py:35
  339.0 30.5 %fusion.102 = f32[256,128,128]{2,1,0:T(8,128)} fusion(f32[256,64,128]{2,1,0:T(8,128)} %bitcast.239, f32[128,128]{0,1:T(8,128)S(1)} %fusion.105), kind=kOutput, calls=%fused_computation.160 | convolution fusion | flops 3221225472 | bytes 25198592 | tf_op jit(solution)/shard_map/kp,bpq->bkq/dot_general | solution.py:88
  369.5 32.9 %fusion.66 = f32[256,128,128]{2,1,0:T(8,128)} fusion(f32[256,128,128]{2,1,0:T(8,128)S(1)} %bitcast.236, f32[256,128,128]{2,1,0:T(8,128)} %fusion.102, f32[128,128]{0,1:T(8,128)S(1)} %get-tuple-element.159, f32[128,128]{0,1:T(8,128)S(1)} %get-tuple-element.160), kind=kOutput, calls=%fused_computation.113 | convolution fusion | flops 6455279616 | bytes 50462720 | tf_op jit(solution)/shard_map/bkq,ql->bkl/dot_general | solution.py:101
  402.4 33.1 %fusion.68 = f32[256,128,128]{2,1,0:T(8,128)} fusion(f32[256,128,128]{2,1,0:T(8,128)S(1)} %bitcast.236, f32[256,128,128]{2,1,0:T(8,128)} %fusion.102, f32[128,128]{0,1:T(8,128)S(1)} %get-tuple-element.159, f32[128,128]{0,1:T(8,128)S(1)} %get-tuple-element.160), kind=kOutput, calls=%fused_computation.114 | convolution fusion | flops 6455263232 | bytes 50462720 | tf_op jit(solution)/shard_map/bkq,ql->bkl/dot_general | solution.py:98
  435.5 34.1 %convolution_add_fusion.3 = f32[256,128,128]{2,1,0:T(8,128)} fusion(f32[256,128,128]{2,1,0:T(8,128)} %fusion.66, f32[256,128,128]{2,1,0:T(8,128)S(1)} %bitcast.236, f32[256,128,128]{2,1,0:T(8,128)} %fusion.102, f32[128,128]{0,1:T(8,128)S(1)} %get-tuple-element.159, f32[128,128]{0,1:T(8,128)S(1)} %get-tuple-element.160), kind=kOutput, calls=%fused_computation.47 | convolution fusion | flops 6459457536 | bytes 67239936 | tf_op jit(solution)/shard_map/bkq,ql->bkl/dot_general | solution.py:101
  469.6 34.1 %convolution_subtract_fusion.1 = f32[256,128,128]{2,1,0:T(8,128)} fusion(f32[256,128,128]{2,1,0:T(8,128)} %fusion.68, f32[256,128,128]{2,1,0:T(8,128)S(1)} %bitcast.236, f32[256,128,128]{2,1,0:T(8,128)} %fusion.102, f32[128,128]{0,1:T(8,128)S(1)} %get-tuple-element.159, f32[128,128]{0,1:T(8,128)S(1)} %get-tuple-element.160), kind=kOutput, calls=%fused_computation.49 | convolution fusion | flops 6459473920 | bytes 67239936 | tf_op jit(solution)/shard_map/bkq,ql->bkl/dot_general | solution.py:98
  537.7 21.2 %convolution_add_fusion.1 = f32[256,128,128]{2,1,0:T(8,128)} fusion(f32[256,128,128]{2,1,0:T(8,128)} %fusion.120, bf16[256,64,128]{2,1,0:T(8,128)(2,1)} %copy.135, f32[128,128]{0,1:T(8,128)S(1)} %fusion.105), kind=kOutput, calls=%fused_computation.44 | convolution fusion | flops 541097984 | bytes 37781504 | tf_op jit(solution)/shard_map/kp,bpq->bkq/dot_general | solution.py:87
  558.9 32.6 %fusion.60 = f32[256,128,128]{2,1,0:T(8,128)} fusion(f32[256,128,128]{2,1,0:T(8,128)S(1)} %convolution_add_fusion, f32[256,128,128]{2,1,0:T(8,128)} %convolution_add_fusion.1, f32[128,128]{0,1:T(8,128)S(1)} %get-tuple-element.159, f32[128,128]{0,1:T(8,128)S(1)} %get-tuple-element.160), kind=kOutput, calls=%fused_computation.111 | convolution fusion | flops 6455279616 | bytes 50462720 | tf_op jit(solution)/shard_map/bkq,ql->bkl/dot_general | solution.py:101
  591.5 32.8 %fusion.62 = f32[256,128,128]{2,1,0:T(8,128)} fusion(f32[256,128,128]{2,1,0:T(8,128)S(1)} %convolution_add_fusion, f32[256,128,128]{2,1,0:T(8,128)} %convolution_add_fusion.1, f32[128,128]{0,1:T(8,128)S(1)} %get-tuple-element.159, f32[128,128]{0,1:T(8,128)S(1)} %get-tuple-element.160), kind=kOutput, calls=%fused_computation.112 | convolution fusion | flops 6455263232 | bytes 50462720 | tf_op jit(solution)/shard_map/bkq,ql->bkl/dot_general | solution.py:98
  624.3 34.1 %convolution_subtract_fusion.2 = f32[256,128,128]{2,1,0:T(8,128)} fusion(f32[256,128,128]{2,1,0:T(8,128)} %fusion.62, f32[256,128,128]{2,1,0:T(8,128)S(1)} %convolution_add_fusion, f32[256,128,128]{2,1,0:T(8,128)} %convolution_add_fusion.1, f32[128,128]{0,1:T(8,128)S(1)} %get-tuple-element.159, f32[128,128]{0,1:T(8,128)S(1)} %get-tuple-element.160), kind=kOutput, calls=%fused_computation.50 | convolution fusion | flops 6459473920 | bytes 67239936 | tf_op jit(solution)/shard_map/bkq,ql->bkl/dot_general | solution.py:98
  658.4 51.1 %multiply_add_fusion = (f32[256,128,128]{2,1,0:T(8,128)}, f32[256,128,128]{2,1,0:T(8,128)}) fusion(f32[256,128,128]{2,1,0:T(8,128)} %convolution_subtract_fusion.1, f32[256,128,128]{2,1,0:T(8,128)} %convolution_subtract_fusion.2, f32[256,128,128]{2,1,0:T(8,128)} %convolution_add_fusion.3, f32[256,128,128]{2,1,0:T(8,128)} %fusion.60, ...), kind=kOutput, calls=%fused_computation.33 | convolution fusion | flops 6484623360 | bytes 134348800 | tf_op jit(solution)/shard_map/bkq,ql->bkl/dot_general | solution.py:101
  709.4 23.2 %fusion.85 = f32[256,128,128]{1,2,0:T(8,128)} fusion(f32[256,128,128]{2,1,0:T(8,128)} %get-tuple-element.127), kind=kOutput, calls=%fused_computation.140 | convolution fusion | flops 6442680320 | bytes 33554432 | tf_op jit(solution)/shard_map/bkl,lq->bkq/dot_general | solution.py:115
  732.7 22.9 %fusion.87 = f32[256,128,128]{1,2,0:T(8,128)} fusion(f32[256,128,128]{2,1,0:T(8,128)} %get-tuple-element.128), kind=kOutput, calls=%fused_computation.142 | convolution fusion | flops 6442680320 | bytes 33554432 | tf_op jit(solution)/shard_map/bkl,lq->bkq/dot_general | solution.py:112
  755.6 24.0 %convolution_subtract_fusion = f32[256,128,128]{1,2,0:T(8,128)} fusion(f32[256,128,128]{1,2,0:T(8,128)} %fusion.85, f32[256,128,128]{2,1,0:T(8,128)} %get-tuple-element.128), kind=kOutput, calls=%fused_computation.45 | convolution fusion | flops 6446891008 | bytes 50331648 | tf_op jit(solution)/shard_map/bkl,lq->bkq/dot_general | solution.py:115
  779.6 23.9 %convolution_add_fusion.2 = f32[256,128,128]{1,2,0:T(8,128)} fusion(f32[256,128,128]{1,2,0:T(8,128)} %fusion.87, f32[256,128,128]{2,1,0:T(8,128)} %get-tuple-element.127), kind=kOutput, calls=%fused_computation.46 | convolution fusion | flops 6446891008 | bytes 50331648 | tf_op jit(solution)/shard_map/bkl,lq->bkq/dot_general | solution.py:112
  803.4 28.4 %fusion.6 = f32[256,128,64]{1,2,0:T(8,128)} fusion(f32[256,128,128]{1,2,0:T(8,128)} %convolution_add_fusion.2, f32[256,128,128]{1,2,0:T(8,128)} %convolution_subtract_fusion, f32[128,128]{0,1:T(8,128)S(1)} %get-tuple-element.159, f32[128,128]{0,1:T(8,128)S(1)} %get-tuple-element.160, f32[128,128]{0,1:T(8,128)S(1)} %copy-done.6), kind=kOutput, calls=%fused_computation.25 | convolution fusion | flops 3233808384 | bytes 42139648 | tf_op jit(solution)/shard_map/pk,bkq->bpq/dot_general | solution.py:122
  831.9 26.7 %multiply_bitcast_fusion = f32[256,64,128]{2,1,0:T(8,128)} fusion(f32[256,128,64]{1,2,0:T(8,128)} %fusion.6, f32[256,128,128]{1,2,0:T(8,128)} %convolution_subtract_fusion, f32[256,128,128]{1,2,0:T(8,128)} %convolution_add_fusion.2, f32[128,128]{0,1:T(8,128)S(1)} %get-tuple-element.159, f32[128,128]{0,1:T(8,128)S(1)} %get-tuple-element.160, ...), kind=kOutput, calls=%fused_computation.105 | convolution fusion | flops 3238002688 | bytes 50528256 | tf_op jit(solution)/shard_map/pk,bkq->bpq/dot_general | solution.py:120
  880.7 175.6 %all-to-all-done.1 = f32[256,16,512]{0,2,1:T(8,128)} async-done(((f32[256,16,512]{0,2,1:T(8,128)}), f32[256,16,512]{0,2,1:T(8,128)}, u32[]{:S(2)}, u32[]{:S(2)}) %all-to-all-start.1) | async-done | bytes 8388640 | tf_op jit(solution)/shard_map/all_to_all | solution.py:179
  (128 shorter events, 262.3 us)
Async XLA Ops:
  0.0 16.6 %copy-start.9 = (s32[512]{0:T(512)S(1)}, s32[512]{0:T(512)}, u32[]{:S(2)}) copy-start(s32[512]{0:T(512)} %param.10) | copy-start | bytes 6148
  16.6 25.8 %copy-start.14 = (f32[7,4096]{1,0:T(8,128)S(1)}, f32[7,4096]{1,0:T(8,128)}, u32[]{:S(2)}) copy-start(f32[7,4096]{1,0:T(8,128)} %param.14) | copy-start | bytes 344068
  16.6 25.9 %copy-start.12 = (f32[3,3,4096]{2,1,0:T(4,128)S(1)}, f32[3,3,4096]{2,1,0:T(4,128)}, u32[]{:S(2)}) copy-start(f32[3,3,4096]{2,1,0:T(4,128)} %param.13) | copy-start | bytes 442372
  16.7 26.0 %copy-start.13 = (f32[3,3,4096]{2,1,0:T(4,128)S(1)}, f32[3,3,4096]{2,1,0:T(4,128)}, u32[]{:S(2)}) copy-start(f32[3,3,4096]{2,1,0:T(4,128)} %param.15) | copy-start | bytes 442372
  38.4 193.4 %collective-permute-start = (bf16[8,3,4096]{2,0,1:T(8,128)(2,1)S(1)}, bf16[8,3,4096]{2,0,1:T(8,128)(2,1)S(1)}, u32[]{:S(2)}, u32[]{:S(2)}) collective-permute-start(bf16[8,3,4096]{2,0,1:T(8,128)(2,1)S(1)} %bitcast.246), channel_id=1, source_target_pairs={{0,2},{2,4},{4,6},{6,8},{8,10},{10,12},{12,14},{14,16},{16,18},{18... | collective-permute-start | bytes 589832 | tf_op jit(solution)/shard_map/ppermute | solution.py:15
  42.4 107.2 %copy-start.4 = (f32[128,128]{0,1:T(8,128)}, f32[128,128]{0,1:T(8,128)S(1)}, u32[]{:S(2)}) copy-start(f32[128,128]{0,1:T(8,128)S(1)} %sine_negate_fusion.1) | copy-start | bytes 196612
  309.3 3.1 collective-permute-start.1
  312.4 16.1 %copy-start.10 = (bf16[2,4096]{1,0:T(2,128)(2,1)}, bf16[2,4096]{1,0:T(2,128)(2,1)S(1)}, u32[]{:S(2)}) copy-start(bf16[2,4096]{1,0:T(2,128)(2,1)S(1)} %collective-permute-done.1) | copy-start | bytes 49156
  330.9 172.8 %all-to-all-start = ((bf16[16,256,512]{1,2,0:T(8,128)(2,1)}), bf16[16,256,512]{1,2,0:T(8,128)(2,1)}, u32[]{:S(2)}, u32[]{:S(2)}) async-start(bf16[16,256,512]{1,2,0:T(8,128)(2,1)} %bitcast.244), calls=%async_computation | async-start | bytes 8388608 | tf_op jit(solution)/shard_map/all_to_all | solution.py:173
  338.7 30.8 %slice-start = ((s8[16777216]{0:T(1024)(128)(4,1)}), s8[4194304]{0:T(1024)(128)(4,1)S(1)}, s32[]{:S(2)}) async-start(s8[16777216]{0:T(1024)(128)(4,1)} %bitcast.235), calls=%async_computation.2 | async-start | bytes 8388608
  339.0 198.7 %copy-start.7 = (f32[128,128]{0,1:T(8,128)}, f32[128,128]{0,1:T(8,128)S(1)}, u32[]{:S(2)}) copy-start(f32[128,128]{0,1:T(8,128)S(1)} %fusion.105) | copy-start | bytes 196612
  339.0 30.5 %slice-start.1 = ((s8[16777216]{0:T(1024)(128)(4,1)}), s8[4194304]{0:T(1024)(128)(4,1)S(1)}, s32[]{:S(2)}) async-start(s8[16777216]{0:T(1024)(128)(4,1)} %bitcast.235), calls=%async_computation.3 | async-start | bytes 8388608
  339.0 30.5 %slice-start.2 = ((s8[16777216]{0:T(1024)(128)(4,1)}), s8[4194304]{0:T(1024)(128)(4,1)S(1)}, s32[]{:S(2)}) async-start(s8[16777216]{0:T(1024)(128)(4,1)} %bitcast.235), calls=%async_computation.4 | async-start | bytes 8388608
  339.0 30.5 %slice-start.3 = ((s8[16777216]{0:T(1024)(128)(4,1)}), s8[4194304]{0:T(1024)(128)(4,1)S(1)}, s32[]{:S(2)}) async-start(s8[16777216]{0:T(1024)(128)(4,1)} %bitcast.235), calls=%async_computation.5 | async-start | bytes 8388608
  469.6 40.7 %copy-start.5 = (f32[128,128]{0,1:T(8,128)S(1)}, f32[128,128]{0,1:T(8,128)}, u32[]{:S(2)}) copy-start(f32[128,128]{0,1:T(8,128)} %copy-done.4) | copy-start | bytes 196612
  510.3 10.5 copy-start.2
  537.7 86.6 %copy-start = (f32[256,128,128]{2,1,0:T(8,128)}, f32[256,128,128]{2,1,0:T(8,128)S(1)}, u32[]{:S(2)}) copy-start(f32[256,128,128]{2,1,0:T(8,128)S(1)} %convolution_add_fusion) | copy-start | bytes 50331652
  779.6 23.9 %copy-start.6 = (f32[128,128]{0,1:T(8,128)S(1)}, f32[128,128]{0,1:T(8,128)}, u32[]{:S(2)}) copy-start(f32[128,128]{0,1:T(8,128)} %copy-done.4) | copy-start | bytes 196612
  803.4 28.4 %copy-start.8 = (f32[128,128]{0,1:T(8,128)S(1)}, f32[128,128]{0,1:T(8,128)}, u32[]{:S(2)}) copy-start(f32[128,128]{0,1:T(8,128)} %copy-done.7) | copy-start | bytes 196612
  867.8 6.2 copy-start.11
  867.8 188.5 %all-to-all-start.1 = ((f32[256,16,512]{0,2,1:T(8,128)}), f32[256,16,512]{0,2,1:T(8,128)}, u32[]{:S(2)}, u32[]{:S(2)}) async-start(f32[256,16,512]{0,2,1:T(8,128)} %bitcast.242), calls=%async_computation.1 | async-start | bytes 16777216 | tf_op jit(solution)/shard_map/all_to_all | solution.py:179
  880.7 183.4 %copy-start.15 = (f32[1,1,4096]{2,1,0:T(1,128)S(1)}, f32[1,1,4096]{2,1,0:T(1,128)}, u32[]{:S(2)}) copy-start(f32[1,1,4096]{2,1,0:T(1,128)} %get-tuple-element.132) | copy-start | bytes 49156
  880.7 183.4 %copy-start.16 = (f32[1,1,4096]{2,1,0:T(1,128)S(1)}, f32[1,1,4096]{2,1,0:T(1,128)}, u32[]{:S(2)}) copy-start(f32[1,1,4096]{2,1,0:T(1,128)} %get-tuple-element.137) | copy-start | bytes 49156
  880.7 183.4 %copy-start.17 = (f32[1,1,4096]{2,1,0:T(1,128)S(1)}, f32[1,1,4096]{2,1,0:T(1,128)}, u32[]{:S(2)}) copy-start(f32[1,1,4096]{2,1,0:T(1,128)} %get-tuple-element.138) | copy-start | bytes 49156
  (2 other events, 7.8 us)
where the time goes:
time: 1090 us; the launch traced here: 1080 us
  matrix products  600 us (55%)
  other arithmetic  177 us (16%)
  waiting for transfers between devices  176 us (16%)
  local copies, waits for them, and re-layouts  104 us (10%)
  starting transfers between devices  19.6 us (2%)
    all_to_all x1, waiting for transfers between devices, on_device(): lax.all_to_all(convolved, 'ctx', split_axis=1, concat_axis=0, tiled=True)  176 us
    add x16, other arithmetic, add_mode(): return summed + weight_col * jnp.exp(-decay_col * positions[None, :])  99.6 us
    dot_general x2, matrix products, forward_transform(): jnp.einsum('bkq,ql->bkl', turned_im, col_re, precision=PRECISE)  85.2 us
    dot_general x2, matrix products, forward_transform(): jnp.einsum('bkq,ql->bkl', turned_im, col_im, precision=PRECISE)  68.2 us
    dot_general x2, matrix products, forward_transform(): jnp.einsum('bkq,ql->bkl', turned_re, col_re, precision=PRECISE)  65.9 us
    dot_general x2, matrix products, forward_transform(): jnp.einsum('bkq,ql->bkl', turned_re, col_im, precision=PRECISE)  65.4 us
    dot_general x2, matrix products, first_section(): return jnp.einsum('kp,bpq->bkq', table, signal, precision=PRECISE)  59.7 us
    dot_general x1, matrix products, look_up(): embedded = jnp.dot(one_hot, embed_table, preferred_element_type=jnp.float32)  36.9 us
  transfers between devices with their start and end apart: 4, of which 2 were waited for; matrix products, arithmetic and copies ran while one was open for 33% of the time, Pallas kernels for 0%

commit v1 on v0

--- a/solution.py
+++ b/solution.py
@@ -7,6 +7,29 @@
 D = 8192
 epsilon = 1e-06
 PRECISE = lax.Precision.HIGHEST
+
+
+def in_blocks(value, dim, size):
+    lengths = value.shape
+    pieces = value.reshape(*lengths[:dim], size, lengths[dim] // size, *lengths[dim + 1 :])
+    return jnp.moveaxis(pieces, dim, 0)
+
+
+def laid_out(tiles, dim):
+    tiles = jnp.moveaxis(tiles, 0, dim)
+    dims = tiles.shape
+    return tiles.reshape(*dims[:dim], dims[dim] * dims[dim + 1], *dims[dim + 2 :])
+
+
+def sent_to_each(x, axis, split_dim, concat_dim):
+    count, place = (lax.axis_size(axis), lax.axis_index(axis))
+    blocks = in_blocks(x, split_dim, count)
+    done = [blocks[place]]
+    for step in range(1, count):
+        sent = blocks[(place + step) % count]
+        done.append(lax.ppermute(sent, axis, [(i, (i + step) % count) for i in range(count)]))
+    blocks = jnp.stack(done)[(place - jnp.arange(count)) % count]
+    return laid_out(blocks, concat_dim)
 
 
 def shifted(value, axis, steps):
@@ -176,7 +199,7 @@
     my_residue = lax.dynamic_slice_in_dim(residue, first_lane, per_device, 0)
     response = mode_response(my_decay, my_residue, gathered.shape[1], 0.0)
     convolved = causal_convolve(gathered, response)
-    carried = lax.all_to_all(convolved, "ctx", split_axis=1, concat_axis=0, tiled=True)
+    carried = sent_to_each(convolved, "ctx", 1, 0)
     mixed_out = queries * jnp.transpose(carried)
     return (widened[lead_two:] + mixed_out).astype(jnp.bfloat16)
 

time: 1090 us -> 1150 us (1.055)
  local copies, waits for them, and re-layouts: 104 us -> 160 us
    all_to_all x1 -> x0, waiting for transfers between devices: 176 us -> none  [on_device(): lax.all_to_all(convolved, 'ctx', split_axis=1, concat_axis=0, tiled=True)]
    ppermute x0 -> x15, waiting for transfers between devices: none -> 170 us  [sent_to_each(): lax.ppermute(sent, axis, [(i, (i + step) % count) for i in range(count)])]
    another operation x0 -> x3, local copies, waits for them, and re-layouts: none -> 40.3 us
    all_to_all x2 -> x0, local copies, waits for them, and re-layouts: 17.1 us -> none  [on_device(): lax.all_to_all(convolved, 'ctx', split_axis=1, concat_axis=0, tiled=True)]
    unnamed x46 -> x102, local copies, waits for them, and re-layouts: 25 us -> 40.5 us
  transfers between devices with their start and end apart: 4 -> 18, of which waited for: 2 -> 10; matrix products, arithmetic and copies ran while one was open for 33% -> 33% of each run, Pallas kernels for 0% -> 0%
where the time goes in v1:
time: 1150 us; the launch traced here: 1140 us
  matrix products  606 us (53%)
  other arithmetic  176 us (15%)
  waiting for transfers between devices  170 us (15%)
  local copies, waits for them, and re-layouts  160 us (14%)
  starting transfers between devices  24.4 us (2%)
    ppermute x15, waiting for transfers between devices, sent_to_each(): lax.ppermute(sent, axis, [(i, (i + step) % count) for i in range(count)])  170 us
    add x16, other arithmetic, add_mode(): return summed + weight_col * jnp.exp(-decay_col * positions[None, :])  100 us
    dot_general x2, matrix products, forward_transform(): jnp.einsum('bkq,ql->bkl', turned_im, col_re, precision=PRECISE)  85.2 us
    dot_general x2, matrix products, forward_transform(): jnp.einsum('bkq,ql->bkl', turned_im, col_im, precision=PRECISE)  68.2 us
    dot_general x2, matrix products, forward_transform(): jnp.einsum('bkq,ql->bkl', turned_re, col_im, precision=PRECISE)  66.6 us
    dot_general x2, matrix products, forward_transform(): jnp.einsum('bkq,ql->bkl', turned_re, col_re, precision=PRECISE)  65.9 us
    dot_general x2, matrix products, first_section(): return jnp.einsum('kp,bpq->bkq', table, signal, precision=PRECISE)  60.8 us
    unnamed x102, local copies, waits for them, and re-layouts  40.5 us
  transfers between devices with their start and end apart: 18, of which 10 were waited for; matrix products, arithmetic and copies ran while one was open for 33% of the time, Pallas kernels for 0%

profile of v1, /device:TPU:15, one launch (start us, length us, event | category | flops | bytes accessed | tf_op | source)
XLA Modules:
  0.0 1141.7 jit_solution(2019299401036185639)
XLA Ops:
  43.8 24.8 %copy.72 = f32[512,12288]{0,1:T(8,128)} copy(f32[512,12288]{1,0:T(8,128)} %fusion.72) | data formatting | bytes 50331648 | tf_op jit(solution)/shard_map/dot_general | solution.py:60
  70.3 100.4 %while.14 = (s32[]{:T(128)}, f32[256,8192]{1,0:T(8,128)}, f32[256,16]{0,1:T(8,128)S(1)}, f32[256,16]{0,1:T(8,128)S(1)}, s32[]{:T(128)}, /*index=5*/s32[]{:T(128)}) while((s32[]{:T(128)}, f32[256,8192]{1,0:T(8,128)}, f32[256,16]{0,1:T(8,128)S(1)}, f32[256,16]{0,1:T(8,128)S(1)}, s32[]{:T(128)}, /*index=5*/s32[]{:T(128)}) %tuple.79), condition=%wide.region_3.0_spmd.clone, body=%wide.region_2.0_spmd.clone.sunk | while | flops 8397059 | bytes 16848984 | solution.py:169
  179.1 25.1 %copy.73 = f32[512,3,4096]{2,0,1:T(8,128)} copy(f32[512,3,4096]{0,2,1:T(8,128)} %bitcast.317) | data formatting | bytes 50331648 | tf_op jit(solution)/shard_map/reshape | solution.py:61
  204.2 30.3 %fusion.100 = f32[256,128,128]{2,1,0:T(8,128)} fusion(f32[256,64,128]{2,1,0:T(8,128)} %bitcast.314, f32[128,128]{0,1:T(8,128)S(1)} %sine_negate_fusion.1), kind=kOutput, calls=%fused_computation.190 | convolution fusion | flops 3221225472 | bytes 25198592 | tf_op jit(solution)/shard_map/kp,bpq->bkq/dot_general | solution.py:111
  252.9 21.2 %fusion.19 = f32[518,4096]{1,0:T(8,128)} fusion(f32[512,3,4096]{2,0,1:T(8,128)} %copy.73, f32[8,3,4096]{2,0,1:T(8,128)S(1)} %convert_element_type.123, f32[4096]{0:T(1024)S(1)} %bitcast.343, f32[4096]{0:T(1024)S(1)} %bitcast.344, f32[4096]{0:T(1024)S(1)} %bitcast.339, f32[4096]{0:T(1024)S(1)} %bitcast.340, f32[4096]{0:T(1024)S(1)} %bitcast.341, ...), kind=kLoop, calls=%fused_computation.57 | loop fusion | flops 36069376 | bytes 34144256 | tf_op jit(solution)/shard_map/mul | solution.py:68
  274.1 39.9 %fusion.46 = bf16[512,4096]{1,0:T(8,128)(2,1)} fusion(f32[518,4096]{1,0:T(8,128)} %fusion.19, f32[518,4096]{1,0:T(8,128)} %get-tuple-element.130, f32[518,4096]{1,0:T(8,128)} %get-tuple-element.131, f32[518,4096]{1,0:T(8,128)} %get-tuple-element.129, bf16[512,4096]{1,0:T(8,128)(2,1)} %param.11, f32[4096]{0:T(1024)S(1)} %bitcast.362, ...), kind=kOutput, calls=%fused_computation.88 | convolution fusion | flops 2191785984 | bytes 92440576 | tf_op jit(solution)/shard_map/dot_general | solution.py:58
  344.4 30.5 %fusion.102 = f32[256,128,128]{2,1,0:T(8,128)} fusion(f32[256,64,128]{2,1,0:T(8,128)} %bitcast.315, f32[128,128]{0,1:T(8,128)S(1)} %copy-done.17), kind=kOutput, calls=%fused_computation.192 | convolution fusion | flops 3221225472 | bytes 25198592 | tf_op jit(solution)/shard_map/kp,bpq->bkq/dot_general | solution.py:111
  374.9 34.1 %fusion.66 = f32[256,128,128]{2,1,0:T(8,128)} fusion(f32[256,128,128]{2,1,0:T(8,128)} %fusion.100, f32[256,128,128]{2,1,0:T(8,128)} %fusion.102, f32[128,128]{0,1:T(8,128)S(1)} %get-tuple-element.175, f32[128,128]{0,1:T(8,128)S(1)} %get-tuple-element.176), kind=kOutput, calls=%fused_computation.114 | convolution fusion | flops 6455279616 | bytes 50462720 | tf_op jit(solution)/shard_map/bkq,ql->bkl/dot_general | solution.py:124
  409.0 33.1 %fusion.68 = f32[256,128,128]{2,1,0:T(8,128)} fusion(f32[256,128,128]{2,1,0:T(8,128)S(1)} %bitcast.312, f32[256,128,128]{2,1,0:T(8,128)} %fusion.102, f32[128,128]{0,1:T(8,128)S(1)} %get-tuple-element.175, f32[128,128]{0,1:T(8,128)S(1)} %get-tuple-element.176), kind=kOutput, calls=%fused_computation.115 | convolution fusion | flops 6455263232 | bytes 50462720 | tf_op jit(solution)/shard_map/bkq,ql->bkl/dot_general | solution.py:121
  442.1 34.1 %convolution_add_fusion.3 = f32[256,128,128]{2,1,0:T(8,128)} fusion(f32[256,128,128]{2,1,0:T(8,128)} %fusion.66, f32[256,128,128]{2,1,0:T(8,128)S(1)} %bitcast.312, f32[256,128,128]{2,1,0:T(8,128)} %fusion.102, f32[128,128]{0,1:T(8,128)S(1)} %get-tuple-element.175, f32[128,128]{0,1:T(8,128)S(1)} %get-tuple-element.176), kind=kOutput, calls=%fused_computation.48 | convolution fusion | flops 6459457536 | bytes 67239936 | tf_op jit(solution)/shard_map/bkq,ql->bkl/dot_general | solution.py:124
  476.2 34.1 %convolution_subtract_fusion.1 = f32[256,128,128]{2,1,0:T(8,128)} fusion(f32[256,128,128]{2,1,0:T(8,128)} %fusion.68, f32[256,128,128]{2,1,0:T(8,128)S(1)} %bitcast.312, f32[256,128,128]{2,1,0:T(8,128)} %fusion.102, f32[128,128]{0,1:T(8,128)S(1)} %get-tuple-element.175, f32[128,128]{0,1:T(8,128)S(1)} %get-tuple-element.176), kind=kOutput, calls=%fused_computation.50 | convolution fusion | flops 6459473920 | bytes 67239936 | tf_op jit(solution)/shard_map/bkq,ql->bkl/dot_general | solution.py:121
  544.3 21.2 %convolution_add_fusion.1 = f32[256,128,128]{2,1,0:T(8,128)} fusion(f32[256,128,128]{2,1,0:T(8,128)} %fusion.120, bf16[256,64,128]{2,1,0:T(8,128)(2,1)} %copy.133, f32[128,128]{0,1:T(8,128)S(1)} %copy-done.17), kind=kOutput, calls=%fused_computation.45 | convolution fusion | flops 541097984 | bytes 37781504 | tf_op jit(solution)/shard_map/kp,bpq->bkq/dot_general | solution.py:110
  565.6 32.6 %fusion.60 = f32[256,128,128]{2,1,0:T(8,128)} fusion(f32[256,128,128]{2,1,0:T(8,128)S(1)} %convolution_add_fusion, f32[256,128,128]{2,1,0:T(8,128)} %convolution_add_fusion.1, f32[128,128]{0,1:T(8,128)S(1)} %get-tuple-element.175, f32[128,128]{0,1:T(8,128)S(1)} %get-tuple-element.176), kind=kOutput, calls=%fused_computation.112 | convolution fusion | flops 6455279616 | bytes 50462720 | tf_op jit(solution)/shard_map/bkq,ql->bkl/dot_general | solution.py:124
  598.1 32.8 %fusion.62 = f32[256,128,128]{2,1,0:T(8,128)} fusion(f32[256,128,128]{2,1,0:T(8,128)S(1)} %convolution_add_fusion, f32[256,128,128]{2,1,0:T(8,128)} %convolution_add_fusion.1, f32[128,128]{0,1:T(8,128)S(1)} %get-tuple-element.175, f32[128,128]{0,1:T(8,128)S(1)} %get-tuple-element.176), kind=kOutput, calls=%fused_computation.113 | convolution fusion | flops 6455263232 | bytes 50462720 | tf_op jit(solution)/shard_map/bkq,ql->bkl/dot_general | solution.py:121
  630.9 34.1 %convolution_subtract_fusion.2 = f32[256,128,128]{2,1,0:T(8,128)} fusion(f32[256,128,128]{2,1,0:T(8,128)} %fusion.62, f32[256,128,128]{2,1,0:T(8,128)S(1)} %convolution_add_fusion, f32[256,128,128]{2,1,0:T(8,128)} %convolution_add_fusion.1, f32[128,128]{0,1:T(8,128)S(1)} %get-tuple-element.175, f32[128,128]{0,1:T(8,128)S(1)} %get-tuple-element.176), kind=kOutput, calls=%fused_computation.51 | convolution fusion | flops 6459473920 | bytes 67239936 | tf_op jit(solution)/shard_map/bkq,ql->bkl/dot_general | solution.py:121
  665.0 51.1 %multiply_add_fusion = (f32[256,128,128]{2,1,0:T(8,128)}, f32[256,128,128]{2,1,0:T(8,128)}) fusion(f32[256,128,128]{2,1,0:T(8,128)} %convolution_subtract_fusion.1, f32[256,128,128]{2,1,0:T(8,128)} %convolution_subtract_fusion.2, f32[256,128,128]{2,1,0:T(8,128)} %convolution_add_fusion.3, f32[256,128,128]{2,1,0:T(8,128)} %fusion.60, ...), kind=kOutput, calls=%fused_computation.34 | convolution fusion | flops 6484623360 | bytes 134348800 | tf_op jit(solution)/shard_map/bkq,ql->bkl/dot_general | solution.py:124
  716.1 23.3 %fusion.85 = f32[256,128,128]{1,2,0:T(8,128)} fusion(f32[256,128,128]{2,1,0:T(8,128)} %get-tuple-element.127), kind=kOutput, calls=%fused_computation.172 | convolution fusion | flops 6442680320 | bytes 33554432 | tf_op jit(solution)/shard_map/bkl,lq->bkq/dot_general | solution.py:138
  739.4 23.0 %fusion.87 = f32[256,128,128]{1,2,0:T(8,128)} fusion(f32[256,128,128]{2,1,0:T(8,128)} %get-tuple-element.128), kind=kOutput, calls=%fused_computation.174 | convolution fusion | flops 6442680320 | bytes 33554432 | tf_op jit(solution)/shard_map/bkl,lq->bkq/dot_general | solution.py:135
  762.4 24.0 %convolution_subtract_fusion = f32[256,128,128]{1,2,0:T(8,128)} fusion(f32[256,128,128]{1,2,0:T(8,128)} %fusion.85, f32[256,128,128]{2,1,0:T(8,128)} %get-tuple-element.128), kind=kOutput, calls=%fused_computation.46 | convolution fusion | flops 6446891008 | bytes 50331648 | tf_op jit(solution)/shard_map/bkl,lq->bkq/dot_general | solution.py:138
  786.4 23.9 %convolution_add_fusion.2 = f32[256,128,128]{1,2,0:T(8,128)} fusion(f32[256,128,128]{1,2,0:T(8,128)} %fusion.87, f32[256,128,128]{2,1,0:T(8,128)} %get-tuple-element.127), kind=kOutput, calls=%fused_computation.47 | convolution fusion | flops 6446891008 | bytes 50331648 | tf_op jit(solution)/shard_map/bkl,lq->bkq/dot_general | solution.py:135
  810.3 28.7 %fusion.6 = f32[256,128,64]{1,2,0:T(8,128)} fusion(f32[256,128,128]{1,2,0:T(8,128)} %convolution_add_fusion.2, f32[256,128,128]{1,2,0:T(8,128)} %convolution_subtract_fusion, f32[128,128]{0,1:T(8,128)S(1)} %get-tuple-element.175, f32[128,128]{0,1:T(8,128)S(1)} %get-tuple-element.176, f32[128,128]{0,1:T(8,128)S(1)} %copy-done.21), kind=kOutput, calls=%fused_computation.26 | convolution fusion | flops 3233808384 | bytes 42139648 | tf_op jit(solution)/shard_map/pk,bkq->bpq/dot_general | solution.py:145
  839.0 26.8 %multiply_bitcast_fusion = f32[256,64,128]{2,1,0:T(8,128)} fusion(f32[256,128,64]{1,2,0:T(8,128)} %fusion.6, f32[256,128,128]{1,2,0:T(8,128)} %convolution_subtract_fusion, f32[256,128,128]{1,2,0:T(8,128)} %convolution_add_fusion.2, f32[128,128]{0,1:T(8,128)S(1)} %get-tuple-element.175, f32[128,128]{0,1:T(8,128)S(1)} %get-tuple-element.176, ...), kind=kOutput, calls=%fused_computation.106 | convolution fusion | flops 3238002688 | bytes 50528256 | tf_op jit(solution)/shard_map/pk,bkq->bpq/dot_general | solution.py:143
  875.2 30.1 %constant_dynamic-slice_fusion.1 = (f32[256,1,512]{2,1,0:T(1,128)}, f32[256,1,512]{2,1,0:T(1,128)}, f32[256,1,512]{2,1,0:T(1,128)}, f32[256,1,512]{2,1,0:T(1,128...) fusion(f32[256,16,512]{2,1,0:T(8,128)} %reshape_reshape.3, ...), kind=kLoop, calls=%fused_computation.220 | loop fusion | bytes 16777280 | tf_op jit(solution)/shard_map/dynamic-slice.15
  955.4 77.4 %collective-permute-done.6 = f32[256,512]{1,0:T(8,128)S(1)} collective-permute-done((f32[256,512]{1,0:T(8,128)S(1)}, f32[256,512]{1,0:T(8,128)S(1)}, u32[]{:S(2)}, u32[]{:S(2)}) %collective-permute-start.6) | collective-permute-done | bytes 524320 | tf_op jit(solution)/shard_map/ppermute | solution.py:30
  (217 shorter events, 404.8 us)
Async XLA Ops:
  38.4 196.4 %collective-permute-start = (bf16[8,3,4096]{2,0,1:T(8,128)(2,1)S(1)}, bf16[8,3,4096]{2,0,1:T(8,128)(2,1)S(1)}, u32[]{:S(2)}, u32[]{:S(2)}) collective-permute-start(bf16[8,3,4096]{2,0,1:T(8,128)(2,1)S(1)} %bitcast.336), channel_id=1, source_target_pairs={{0,2},{2,4},{4,6},{6,8},{8,10},{10,12},{12,14},{14,16},{16,18},{18... | collective-permute-start | bytes 589832 | tf_op jit(solution)/shard_map/ppermute | solution.py:38
  43.8 160.4 %copy-start.19 = (f32[128,128]{0,1:T(8,128)}, f32[128,128]{0,1:T(8,128)S(1)}, u32[]{:S(2)}) copy-start(f32[128,128]{0,1:T(8,128)S(1)} %sine_negate_fusion.1) | copy-start | bytes 196612
  314.8 3.1 collective-permute-start.1
  336.5 173.7 %all-to-all-start = ((bf16[16,256,512]{1,2,0:T(8,128)(2,1)}), bf16[16,256,512]{1,2,0:T(8,128)(2,1)}, u32[]{:S(2)}, u32[]{:S(2)}) async-start(bf16[16,256,512]{1,2,0:T(8,128)(2,1)} %bitcast.319), calls=%async_computation | async-start | bytes 8388608 | tf_op jit(solution)/shard_map/all_to_all | solution.py:196
  344.4 64.6 %slice-start = ((s8[16777216]{0:T(1024)(128)(4,1)}), s8[4194304]{0:T(1024)(128)(4,1)S(1)}, s32[]{:S(2)}) async-start(s8[16777216]{0:T(1024)(128)(4,1)} %bitcast.311), calls=%async_computation.1 | async-start | bytes 8388608
  344.4 64.6 %slice-start.1 = ((s8[16777216]{0:T(1024)(128)(4,1)}), s8[4194304]{0:T(1024)(128)(4,1)S(1)}, s32[]{:S(2)}) async-start(s8[16777216]{0:T(1024)(128)(4,1)} %bitcast.311), calls=%async_computation.2 | async-start | bytes 8388608
  476.2 40.7 %copy-start.20 = (f32[128,128]{0,1:T(8,128)S(1)}, f32[128,128]{0,1:T(8,128)}, u32[]{:S(2)}) copy-start(f32[128,128]{0,1:T(8,128)} %copy-done.19) | copy-start | bytes 196612
  544.3 86.6 %copy-start = (f32[256,128,128]{2,1,0:T(8,128)}, f32[256,128,128]{2,1,0:T(8,128)S(1)}, u32[]{:S(2)}) copy-start(f32[256,128,128]{2,1,0:T(8,128)S(1)} %convolution_add_fusion) | copy-start | bytes 50331652
  875.2 35.2 %copy-start.24 = (bf16[2,4096]{1,0:T(2,128)(2,1)S(1)}, bf16[2,4096]{1,0:T(2,128)(2,1)}, u32[]{:S(2)}) copy-start(bf16[2,4096]{1,0:T(2,128)(2,1)} %copy-done.23) | copy-start | bytes 49156
  907.7 13.1 %collective-permute-start.2 = (f32[256,512]{1,0:T(8,128)S(1)}, f32[256,512]{1,0:T(8,128)S(1)}, u32[]{:S(2)}, u32[]{:S(2)}) collective-permute-start(f32[256,512]{1,0:T(8,128)S(1)} %bitcast.335), channel_id=1, source_target_pairs={{0,2},{2,4},{4,6},{6,8},{8,10},{10,12},{12,14},{14,16},{16,18},{18... | collective-permute-start | bytes 1572872 | tf_op jit(solution)/shard_map/ppermute | solution.py:30
  909.4 22.7 %collective-permute-start.3 = (f32[256,512]{1,0:T(8,128)S(1)}, f32[256,512]{1,0:T(8,128)S(1)}, u32[]{:S(2)}, u32[]{:S(2)}) collective-permute-start(f32[256,512]{1,0:T(8,128)S(1)} %bitcast.332), channel_id=1, source_target_pairs={{0,4},{2,6},{4,8},{6,10},{8,12},{10,14},{12,16},{14,18},{16,20},{1... | collective-permute-start | bytes 1572872 | tf_op jit(solution)/shard_map/ppermute | solution.py:30
  915.1 27.8 %collective-permute-start.4 = (f32[256,512]{1,0:T(8,128)S(1)}, f32[256,512]{1,0:T(8,128)S(1)}, u32[]{:S(2)}, u32[]{:S(2)}) collective-permute-start(f32[256,512]{1,0:T(8,128)S(1)} %bitcast.333), channel_id=1, source_target_pairs={{0,6},{2,8},{4,10},{6,12},{8,14},{10,16},{12,18},{14,20},{16,22},{... | collective-permute-start | bytes 1572872 | tf_op jit(solution)/shard_map/ppermute | solution.py:30
  915.6 39.0 %collective-permute-start.5 = (f32[256,512]{1,0:T(8,128)S(1)}, f32[256,512]{1,0:T(8,128)S(1)}, u32[]{:S(2)}, u32[]{:S(2)}) collective-permute-start(f32[256,512]{1,0:T(8,128)S(1)} %bitcast.330), channel_id=1, source_target_pairs={{0,8},{2,10},{4,12},{6,14},{8,16},{10,18},{12,20},{14,22},{16,24},... | collective-permute-start | bytes 1572872 | tf_op jit(solution)/shard_map/ppermute | solution.py:30
  916.4 116.4 %collective-permute-start.6 = (f32[256,512]{1,0:T(8,128)S(1)}, f32[256,512]{1,0:T(8,128)S(1)}, u32[]{:S(2)}, u32[]{:S(2)}) collective-permute-start(f32[256,512]{1,0:T(8,128)S(1)} %bitcast.328), channel_id=1, source_target_pairs={{0,10},{2,12},{4,14},{6,16},{8,18},{10,20},{12,22},{14,24},{16,26}... | collective-permute-start | bytes 1572872 | tf_op jit(solution)/shard_map/ppermute | solution.py:30
  920.7 128.9 %collective-permute-start.7 = (f32[256,512]{1,0:T(8,128)S(1)}, f32[256,512]{1,0:T(8,128)S(1)}, u32[]{:S(2)}, u32[]{:S(2)}) collective-permute-start(f32[256,512]{1,0:T(8,128)S(1)} %bitcast.334), channel_id=1, source_target_pairs={{0,12},{2,14},{4,16},{6,18},{8,20},{10,22},{12,24},{14,26},{16,28}... | collective-permute-start | bytes 1572872 | tf_op jit(solution)/shard_map/ppermute | solution.py:30
  932.1 134.4 %collective-permute-start.8 = (f32[256,512]{1,0:T(8,128)S(1)}, f32[256,512]{1,0:T(8,128)S(1)}, u32[]{:S(2)}, u32[]{:S(2)}) collective-permute-start(f32[256,512]{1,0:T(8,128)S(1)} %bitcast.331), channel_id=1, source_target_pairs={{0,14},{2,16},{4,18},{6,20},{8,22},{10,24},{12,26},{14,28},{16,30}... | collective-permute-start | bytes 1572872 | tf_op jit(solution)/shard_map/ppermute | solution.py:30
  942.9 140.4 %collective-permute-start.9 = (f32[256,512]{1,0:T(8,128)S(1)}, f32[256,512]{1,0:T(8,128)S(1)}, u32[]{:S(2)}, u32[]{:S(2)}) collective-permute-start(f32[256,512]{1,0:T(8,128)S(1)} %bitcast.329), channel_id=1, source_target_pairs={{0,16},{2,18},{4,20},{6,22},{8,24},{10,26},{12,28},{14,30},{16,0},... | collective-permute-start | bytes 1572872 | tf_op jit(solution)/shard_map/ppermute | solution.py:30
  954.6 129.6 %collective-permute-start.10 = (f32[256,512]{1,0:T(8,128)S(1)}, f32[256,512]{1,0:T(8,128)S(1)}, u32[]{:S(2)}, u32[]{:S(2)}) collective-permute-start(f32[256,512]{1,0:T(8,128)S(1)} %bitcast.327), channel_id=1, source_target_pairs={{0,18},{2,20},{4,22},{6,24},{8,26},{10,28},{12,30},{14,0},{16,2},{... | collective-permute-start | bytes 1572872 | tf_op jit(solution)/shard_map/ppermute | solution.py:30
  1032.8 52.2 %collective-permute-start.11 = (f32[256,512]{1,0:T(8,128)S(1)}, f32[256,512]{1,0:T(8,128)S(1)}, u32[]{:S(2)}, u32[]{:S(2)}) collective-permute-start(f32[256,512]{1,0:T(8,128)S(1)} %bitcast.326), channel_id=1, source_target_pairs={{0,20},{2,22},{4,24},{6,26},{8,28},{10,30},{12,0},{14,2},{16,4},{1... | collective-permute-start | bytes 1572872 | tf_op jit(solution)/shard_map/ppermute | solution.py:30
  1049.6 36.5 %collective-permute-start.12 = (f32[256,512]{1,0:T(8,128)S(1)}, f32[256,512]{1,0:T(8,128)S(1)}, u32[]{:S(2)}, u32[]{:S(2)}) collective-permute-start(f32[256,512]{1,0:T(8,128)S(1)} %bitcast.325), channel_id=1, source_target_pairs={{0,22},{2,24},{4,26},{6,28},{8,30},{10,0},{12,2},{14,4},{16,6},{18... | collective-permute-start | bytes 1572872 | tf_op jit(solution)/shard_map/ppermute | solution.py:30
  1066.5 20.5 %collective-permute-start.13 = (f32[256,512]{1,0:T(8,128)S(1)}, f32[256,512]{1,0:T(8,128)S(1)}, u32[]{:S(2)}, u32[]{:S(2)}) collective-permute-start(f32[256,512]{1,0:T(8,128)S(1)} %bitcast.324), channel_id=1, source_target_pairs={{0,24},{2,26},{4,28},{6,30},{8,0},{10,2},{12,4},{14,6},{16,8},{18,... | collective-permute-start | bytes 1572872 | tf_op jit(solution)/shard_map/ppermute | solution.py:30
  1083.4 10.5 collective-permute-start.14
  1084.2 20.9 %collective-permute-start.15 = (f32[256,512]{1,0:T(8,128)S(1)}, f32[256,512]{1,0:T(8,128)S(1)}, u32[]{:S(2)}, u32[]{:S(2)}) collective-permute-start(f32[256,512]{1,0:T(8,128)S(1)} %bitcast.322), channel_id=1, source_target_pairs={{0,28},{2,30},{4,0},{6,2},{8,4},{10,6},{12,8},{14,10},{16,12},{18,... | collective-permute-start | bytes 1572872 | tf_op jit(solution)/shard_map/ppermute | solution.py:30
  1085.0 20.9 %collective-permute-start.16 = (f32[256,512]{1,0:T(8,128)S(1)}, f32[256,512]{1,0:T(8,128)S(1)}, u32[]{:S(2)}, u32[]{:S(2)}) collective-permute-start(f32[256,512]{1,0:T(8,128)S(1)} %bitcast.321), channel_id=1, source_target_pairs={{0,30},{2,0},{4,2},{6,4},{8,6},{10,8},{12,10},{14,12},{16,14},{18,... | collective-permute-start | bytes 1572872 | tf_op jit(solution)/shard_map/ppermute | solution.py:30
  (29 other events, 447.5 us)
